TPU v7x, 128 devices: a whole 4x4x4 slice. The times are simulated.
128 devices in a mesh: seq: 32 (over z, x, core), dp: 4 (over y).
Axes of the slice: x: 4, y: 4, z: 4, core: 2. Of those that a mesh axis runs over, the one named last changes fastest.
Arguments:
- queries: bfloat16 [4, 8192, 1024], P('dp', 'seq'), may hold values from -8 to 8
- key_rows: bfloat16 [4, 8192, 1024], P('dp', 'seq'), may hold values from -8 to 8
- value_rows: bfloat16 [4, 8192, 1024], P('dp', 'seq'), may hold values from -16 to 16
- conv_key: float32 [5, 4, 1024], replicated, may hold values from -2.5 to 2.5
- conv_value: float32 [5, 4, 1024], replicated, may hold values from -2.5 to 2.5
- grad_out: bfloat16 [4, 8192, 1024], P('dp', 'seq'), may hold values from -12 to 12
Outputs:
- attended: bfloat16 [4, 8192, 1024], P('dp', 'seq')
- grad_query: bfloat16 [4, 8192, 1024], P('dp', 'seq')
- grad_key: bfloat16 [4, 8192, 1024], P('dp', 'seq')
- grad_value: bfloat16 [4, 8192, 1024], P('dp', 'seq')
- grad_conv_key: float32 [5, 4, 1024], replicated
- grad_conv_value: float32 [5, 4, 1024], replicated
All inputs are finite; a program needn't handle non-finite values.
Results may differ from a plain program's by a relative error of at most 0.019.
Values may be sent and summed in bfloat16 or wider, within the bound.
No kernel may reach another device: no remote copies, remote signals or barrier semaphores. Data moves between devices by JAX's collectives and lax.ppermute only.
A program may use at most 128 MiB of HBM per device.

v0:
```python
import jax
import jax.numpy as jnp
from jax import lax
from jax.sharding import PartitionSpec as P

HEADS = 8
HEAD_DIM = 128
BLOCK = 128


def passed_along(value, axis, steps):
    count = lax.axis_size(axis)
    initial, last = (max(0, -steps), min(count, count - steps))
    return lax.ppermute(value, axis, [(source, source + steps) for source in range(initial, last)])


def partner_2(array, axis, distance):
    return lax.ppermute(array, axis, [(i, i ^ 1 << distance) for i in range(lax.axis_size(axis))])


def coarsen(extended, weight):
    out_rows = (extended.shape[1] - 2) // 2
    summed = weight[0] * extended[:, 0 : 2 * out_rows : 2].astype(jnp.float32)
    for offset in range(1, 4):
        summed = summed + weight[offset] * extended[:, offset : offset + 2 * out_rows : 2].astype(
            jnp.float32
        )
    return summed.astype(jnp.bfloat16)


def coarsen_back(upstream, extended, weight):
    seqs_dev, out_rows, feat_width = upstream.shape
    zero_row = jnp.zeros((seqs_dev, 1, feat_width), jnp.float32)
    even_rows = jnp.concatenate([weight[0] * upstream, zero_row], 1) + jnp.concatenate(
        [zero_row, weight[2] * upstream], 1
    )
    odd_rows = jnp.concatenate([weight[1] * upstream, zero_row], 1) + jnp.concatenate(
        [zero_row, weight[3] * upstream], 1
    )
    spread = jnp.stack([even_rows, odd_rows], 2).reshape(seqs_dev, 2 * out_rows + 2, feat_width)
    weight_grad = jnp.stack(
        [
            jnp.sum(
                upstream * extended[:, offset : offset + 2 * out_rows : 2].astype(jnp.float32),
                (0, 1),
            )
            for offset in range(4)
        ]
    )
    return (spread, weight_grad)


def move_near(moved_rows, shift_by):
    return passed_along(moved_rows, "seq", shift_by)


def move_grads(moved_rows, shift_by):
    return passed_along(moved_rows.astype(jnp.bfloat16), "seq", shift_by).astype(moved_rows.dtype)


def per_device(queries, key_rows, value_rows, conv_key, conv_value, grad_out):
    seqs_dev, tok_rows, feat_width = queries.shape
    levels = conv_key.shape[0]
    head_count = HEADS
    head_size = HEAD_DIM
    blk_rows = BLOCK
    blocks_here = tok_rows // blk_rows
    local_top = blocks_here.bit_length() - 1
    seq_devices = lax.axis_size("seq")
    dev_index = lax.axis_index("seq")
    total_blocks = blocks_here * seq_devices
    score_scale = head_size ** (-0.5)
    pair_width = 2 * feat_width
    group_heads = 2
    kv_weight = jnp.stack(
        [
            conv_key.reshape(levels, 4, head_count, head_size),
            conv_value.reshape(levels, 4, head_count, head_size),
        ],
        3,
    ).reshape(levels, 4, pair_width)
    fine_pairs = jnp.stack(
        [
            key_rows.reshape(seqs_dev, tok_rows, head_count, head_size),
            value_rows.reshape(seqs_dev, tok_rows, head_count, head_size),
        ],
        3,
    ).reshape(seqs_dev, tok_rows, pair_width)
    own_rows = [fine_pairs]
    left_rims = [move_near(fine_pairs[:, -blk_rows:], 1)]
    right_rims = [move_near(fine_pairs[:, :blk_rows], -1)]
    extended_local = [None]
    level_id = 1
    extended = jnp.concatenate([left_rims[level_id - 1][:, -2:], own_rows[level_id - 1]], 1)
    extended_local.append(extended)
    coarse = coarsen(extended, kv_weight[level_id - 1])
    own_rows.append(coarse)
    left_rims.append(move_near(coarse, 1))
    right_rims.append(move_near(coarse, -1))
    block_now = own_rows[local_top]
    left_now = left_rims[local_top]
    group_lefts, group_rights, group_extended, group_first = ([], [], [], [])
    for level_id in range(local_top + 1, levels + 1):
        swap_bit = level_id - local_top - 1
        extended = jnp.concatenate([left_now[:, -2:], block_now], 1)
        group_extended.append(extended)
        own_half = coarsen(extended, kv_weight[level_id - 1])
        partner = partner_2(own_half, "seq", swap_bit)
        is_first = dev_index // 2**swap_bit % 2 == 0
        group_first.append(is_first)
        block_now = jnp.where(
            is_first,
            jnp.concatenate([own_half, partner], 1),
            jnp.concatenate([partner, own_half], 1),
        )
        stride_dev = 2 ** (level_id - local_top)
        left_now = move_near(block_now, stride_dev)
        right_now = move_near(block_now, -stride_dev)
        group_lefts.append(left_now)
        group_rights.append(right_now)
    glob_blocks = dev_index * blocks_here + jnp.arange(blocks_here, dtype=jnp.int32)
    always = jnp.ones((blocks_here,), jnp.bool_)
    sources = []
    pieces = []
    for level_id in range(local_top + 1):
        block_count = blocks_here >> level_id
        padded = jnp.concatenate([left_rims[level_id], own_rows[level_id], right_rims[level_id]], 1)
        sources.append(
            padded.reshape(seqs_dev, block_count + 2, blk_rows, head_count, 2, head_size)
        )
        coarse_id = glob_blocks // 2**level_id
        spread = 2**level_id
        pieces.append((level_id, 0, spread, coarse_id >= 1))
        if level_id == 0:
            pieces.append((0, 1, 1, always))
        pieces.append((level_id, 2, spread, coarse_id + 1 < total_blocks // 2**level_id))
    for slot_id in range(levels - local_top):
        level_id = local_top + 1 + slot_id
        coarse_id = glob_blocks // 2**level_id
        sources.append(
            group_lefts[slot_id].reshape(seqs_dev, 1, blk_rows, head_count, 2, head_size)
        )
        pieces.append((len(sources) - 1, 0, blocks_here, coarse_id >= 1))
        sources.append(
            group_rights[slot_id].reshape(seqs_dev, 1, blk_rows, head_count, 2, head_size)
        )
        pieces.append(
            (len(sources) - 1, 0, blocks_here, coarse_id + 1 < total_blocks // 2**level_id)
        )
    query_blocks = queries.reshape(seqs_dev, blocks_here, blk_rows, head_count, head_size)
    out_blocks = grad_out.reshape(seqs_dev, blocks_here, blk_rows, head_count, head_size)

    def head_group(group_id, loop_state):
        attended_acc, grad_q_acc, source_grads, log_totals, row_deltas = loop_state
        head_start = group_id * group_heads
        q_part = lax.dynamic_slice_in_dim(query_blocks, head_start, group_heads, 3)
        do_part = lax.dynamic_slice_in_dim(out_blocks, head_start, group_heads, 3)
        source_parts = [
            lax.dynamic_slice_in_dim(source, head_start, group_heads, 3) for source in sources
        ]
        score_list = []
        views = []
        for source_id, offset, spread, valid_mask in pieces:
            block_count = blocks_here // spread
            key_blocks = source_parts[source_id][:, offset : offset + block_count]
            q_view = q_part.reshape(seqs_dev, block_count, spread, blk_rows, group_heads, head_size)
            do_view = do_part.reshape(
                seqs_dev, block_count, spread, blk_rows, group_heads, head_size
            )
            raw_scores = jnp.einsum(
                "bnrqhe,bnkhe->bnrhqk",
                q_view,
                key_blocks[..., 0, :],
                preferred_element_type=jnp.float32,
            )
            raw_scores = (
                raw_scores.reshape(seqs_dev, blocks_here, group_heads, blk_rows, blk_rows)
                * score_scale
            )
            score_list.append(
                jnp.where(valid_mask[None, :, None, None, None], raw_scores, -jnp.inf)
            )
            views.append((key_blocks, q_view, do_view, block_count, spread))
        all_scores = jnp.concatenate(score_list, 4)
        row_max = jnp.max(all_scores, 4, keepdims=True)
        exp_scores = jnp.exp(all_scores - row_max)
        summed = jnp.sum(exp_scores, 4, keepdims=True)
        prob_full = exp_scores / summed
        probs_low = prob_full.astype(jnp.bfloat16)
        attended_part = jnp.zeros(
            (seqs_dev, blocks_here, blk_rows, group_heads, head_size), jnp.float32
        )
        grad_prob_list = []
        for piece_id, (key_blocks, q_view, do_view, block_count, spread) in enumerate(views):
            p_slice = probs_low[..., piece_id * blk_rows : (piece_id + 1) * blk_rows].reshape(
                seqs_dev, block_count, spread, group_heads, blk_rows, blk_rows
            )
            attended_part = attended_part + jnp.einsum(
                "bnrhqk,bnkhe->bnrqhe",
                p_slice,
                key_blocks[..., 1, :],
                preferred_element_type=jnp.float32,
            ).reshape(attended_part.shape)
            grad_prob = jnp.einsum(
                "bnrqhe,bnkhe->bnrhqk",
                do_view,
                key_blocks[..., 1, :],
                preferred_element_type=jnp.float32,
            )
            grad_prob_list.append(
                grad_prob.reshape(seqs_dev, blocks_here, group_heads, blk_rows, blk_rows)
            )
        grad_prob_all = jnp.concatenate(grad_prob_list, 4)
        row_delta = jnp.sum(prob_full * grad_prob_all, 4, keepdims=True)
        dscore = (prob_full * (grad_prob_all - row_delta) * score_scale).astype(jnp.bfloat16)
        grad_q_part = jnp.zeros(
            (seqs_dev, blocks_here, blk_rows, group_heads, head_size), jnp.float32
        )
        group_grads = [jnp.zeros(part_arr.shape, jnp.float32) for part_arr in source_parts]
        for piece_id, (key_blocks, q_view, do_view, block_count, spread) in enumerate(views):
            source_id, offset = (pieces[piece_id][0], pieces[piece_id][1])
            p_slice = probs_low[..., piece_id * blk_rows : (piece_id + 1) * blk_rows].reshape(
                seqs_dev, block_count, spread, group_heads, blk_rows, blk_rows
            )
            ds_slice = dscore[..., piece_id * blk_rows : (piece_id + 1) * blk_rows].reshape(
                seqs_dev, block_count, spread, group_heads, blk_rows, blk_rows
            )
            grad_q_part = grad_q_part + jnp.einsum(
                "bnrhqk,bnkhe->bnrqhe",
                ds_slice,
                key_blocks[..., 0, :],
                preferred_element_type=jnp.float32,
            ).reshape(grad_q_part.shape)
            key_grad = jnp.einsum(
                "bnrhqk,bnrqhe->bnkhe", ds_slice, q_view, preferred_element_type=jnp.float32
            )
            value_grad = jnp.einsum(
                "bnrhqk,bnrqhe->bnkhe", p_slice, do_view, preferred_element_type=jnp.float32
            )
            pair_grad = jnp.stack([key_grad, value_grad], 4)
            group_grads[source_id] = (
                group_grads[source_id].at[:, offset : offset + block_count].add(pair_grad)
            )
        attended_acc = lax.dynamic_update_slice_in_dim(
            attended_acc, attended_part.astype(jnp.bfloat16), head_start, 3
        )
        grad_q_acc = lax.dynamic_update_slice_in_dim(
            grad_q_acc, grad_q_part.astype(jnp.bfloat16), head_start, 3
        )
        source_grads = tuple(
            (
                lax.dynamic_update_slice_in_dim(whole, group_part, head_start, 3)
                for whole, group_part in zip(source_grads, group_grads)
            )
        )
        log_totals = lax.dynamic_update_slice_in_dim(
            log_totals, (row_max + jnp.log(summed))[..., 0], head_start, 2
        )
        row_deltas = lax.dynamic_update_slice_in_dim(row_deltas, row_delta[..., 0], head_start, 2)
        return (attended_acc, grad_q_acc, source_grads, log_totals, row_deltas)

    start_state = (
        jnp.zeros((seqs_dev, blocks_here, blk_rows, head_count, head_size), jnp.bfloat16),
        jnp.zeros((seqs_dev, blocks_here, blk_rows, head_count, head_size), jnp.bfloat16),
        tuple((jnp.zeros(source.shape, jnp.float32) for source in sources)),
        jnp.zeros((seqs_dev, blocks_here, head_count, blk_rows), jnp.float32),
        jnp.zeros((seqs_dev, blocks_here, head_count, blk_rows), jnp.float32),
    )
    attended_acc, grad_q_acc, source_grads, log_totals, row_deltas = lax.fori_loop(
        0, head_count // group_heads, head_group, start_state
    )
    attended = attended_acc.reshape(seqs_dev, tok_rows, feat_width)
    grad_query = grad_q_acc.reshape(seqs_dev, tok_rows, feat_width)
    grad_left, grad_own, grad_right = ([], [], [])
    for level_id in range(local_top + 1):
        flat_grad = source_grads[level_id].reshape(seqs_dev, -1, pair_width)
        grad_left.append(flat_grad[:, :blk_rows])
        grad_own.append(flat_grad[:, blk_rows:-blk_rows])
        grad_right.append(flat_grad[:, -blk_rows:])
    group_left_grads = [
        source_grads[local_top + 1 + 2 * slot_id].reshape(seqs_dev, blk_rows, pair_width)
        for slot_id in range(levels - local_top)
    ]
    group_right_grads = [
        source_grads[local_top + 2 + 2 * slot_id].reshape(seqs_dev, blk_rows, pair_width)
        for slot_id in range(levels - local_top)
    ]
    weight_grads = [None] * levels
    carry_block = jnp.zeros((seqs_dev, blk_rows, pair_width), jnp.float32)
    carry_left = jnp.zeros((seqs_dev, 2, pair_width), jnp.float32)
    for level_id in range(levels, local_top, -1):
        slot_id = level_id - local_top - 1
        stride_dev = 2 ** (level_id - local_top)
        left_total = group_left_grads[slot_id].at[:, -2:].add(carry_left)
        block_total = (
            carry_block
            + move_grads(left_total, -stride_dev)
            + move_grads(group_right_grads[slot_id], stride_dev)
        )
        first_part = block_total[:, : blk_rows // 2]
        second_part = block_total[:, blk_rows // 2 :]
        keep_part = jnp.where(group_first[slot_id], first_part, second_part)
        give_part = jnp.where(group_first[slot_id], second_part, first_part)
        half_grad = keep_part + partner_2(give_part.astype(jnp.bfloat16), "seq", slot_id).astype(
            give_part.dtype
        )
        spread, weight_grads[level_id - 1] = coarsen_back(
            half_grad, group_extended[slot_id], kv_weight[level_id - 1]
        )
        carry_left = spread[:, :2]
        carry_block = spread[:, 2:]
    grad_left[local_top] = grad_left[local_top].at[:, -2:].add(carry_left)
    grad_own[local_top] = grad_own[local_top] + carry_block
    fine_left_conv = jnp.zeros((seqs_dev, blk_rows, pair_width), jnp.float32)
    level_id = 1
    from_right = move_grads(grad_left[level_id], -1)
    from_left = move_grads(grad_right[level_id], 1)
    level_grad = (
        grad_own[level_id].at[:, :blk_rows].add(from_left).at[:, -blk_rows:].add(from_right)
    )
    spread, weight_grads[level_id - 1] = coarsen_back(
        level_grad, extended_local[level_id], kv_weight[level_id - 1]
    )
    fine_left_conv = fine_left_conv.at[:, -2:].add(spread[:, :2])
    grad_own[level_id - 1] = grad_own[level_id - 1] + spread[:, 2:]
    from_right = move_grads(grad_left[0] + fine_left_conv, -1)
    from_left = move_grads(grad_right[0], 1)
    fine_grad = grad_own[0].at[:, :blk_rows].add(from_left).at[:, -blk_rows:].add(from_right)
    grad_pairs = fine_grad.reshape(seqs_dev, tok_rows, head_count, 2, head_size)
    grad_key = (
        grad_pairs[:, :, :, 0, :].reshape(seqs_dev, tok_rows, feat_width).astype(jnp.bfloat16)
    )
    grad_value = (
        grad_pairs[:, :, :, 1, :].reshape(seqs_dev, tok_rows, feat_width).astype(jnp.bfloat16)
    )
    weight_sum = lax.psum(jnp.stack(weight_grads), ("seq", "dp")).reshape(
        levels, 4, head_count, 2, head_size
    )
    grad_conv_key = weight_sum[:, :, :, 0, :].reshape(levels, 4, feat_width)
    grad_conv_value = weight_sum[:, :, :, 1, :].reshape(levels, 4, feat_width)
    return (attended, grad_query, grad_key, grad_value, grad_conv_key, grad_conv_value)


def solution(mesh):
    in_specs = (
        P("dp", "seq", None),
        P("dp", "seq", None),
        P("dp", "seq", None),
        P(),
        P(),
        P("dp", "seq", None),
    )
    out_specs = (
        P("dp", "seq", None),
        P("dp", "seq", None),
        P("dp", "seq", None),
        P("dp", "seq", None),
        P(),
        P(),
    )
    return jax.shard_map(
        per_device, mesh=mesh, in_specs=in_specs, out_specs=out_specs, check_vma=False
    )
```

profile of v0, /device:TPU:1, one launch (start us, length us, event | category | flops | bytes accessed | tf_op | source)
XLA Modules:
  0.0 1245.0 jit_solution(9767372504227561443)
XLA Ops:
  10.7 4.5 collective-permute-start
  15.2 20.2 %slice.1813 = bf16[1,128,2048]{1,2,0:T(8,128)(2,1)S(1)} slice(bf16[1,256,2048]{1,2,0:T(8,128)(2,1)S(1)} %bitcast.1716), slice={[0:1:1], [0:256:2], [0:2048:1]} | slice | bytes 1048576 | tf_op jit(solution)/shard_map/slice | solution.py:25
  35.5 20.2 %slice.1815 = bf16[1,128,2048]{1,2,0:T(8,128)(2,1)S(1)} slice(bf16[1,256,2048]{1,2,0:T(8,128)(2,1)S(1)} %bitcast.1717), slice={[0:1:1], [1:256:2], [0:2048:1]} | slice | bytes 1048576 | tf_op jit(solution)/shard_map/slice | solution.py:25
  58.7 20.9 %slice.1811 = bf16[1,128,2048]{1,2,0:T(8,128)(2,1)S(1)} slice(bf16[1,258,2048]{1,2,0:T(8,128)(2,1)} %pad_maximum_fusion.14), slice={[0:1:1], [1:257:2], [0:2048:1]} | slice | bytes 1048576 | tf_op jit(solution)/shard_map/slice | solution.py:25
  79.6 21.3 %slice.1809 = bf16[1,128,2048]{1,2,0:T(8,128)(2,1)} slice(bf16[1,258,2048]{1,2,0:T(8,128)(2,1)} %pad_maximum_fusion.14), slice={[0:1:1], [0:256:2], [0:2048:1]} | slice | bytes 1048576 | tf_op jit(solution)/shard_map/slice | solution.py:23
  106.1 11.0 slice.1824
  117.1 10.9 slice.1822
  130.9 11.6 slice.1820
  142.4 11.9 slice.1818
  166.5 11.0 slice.1833
  177.5 10.9 slice.1831
  191.2 11.9 slice.1829
  203.2 11.8 slice.1827
  218.9 12.9 %collective-permute-done.7 = bf16[1,64,2048]{1,2,0:T(8,128)(2,1)S(1)} collective-permute-done((bf16[1,64,2048]{1,2,0:T(8,128)(2,1)}, bf16[1,64,2048]{1,2,0:T(8,128)(2,1)S(1)}, u32[]{:S(2)}, u32[]{:S(2)}) %collective-permute-start.7) | collective-permute-done | bytes 262176 | tf_op jit(solution)/shard_map/ppermute | solution.py:18
  233.6 5.2 collective-permute-start.8
  238.8 11.0 slice.1842
  249.8 11.2 slice.1840
  263.7 11.9 slice.1838
  275.6 11.8 slice.1836
  287.4 4.0 fusion.185
  292.2 12.7 %collective-permute-done.10 = bf16[1,64,2048]{1,2,0:T(8,128)(2,1)S(1)} collective-permute-done((bf16[1,64,2048]{1,2,0:T(8,128)(2,1)}, bf16[1,64,2048]{1,2,0:T(8,128)(2,1)S(1)}, u32[]{:S(2)}, u32[]{:S(2)}) %collective-permute-start.10) | collective-permute-done | bytes 262176 | tf_op jit(solution)/shard_map/ppermute | solution.py:18
  310.9 4.8 collective-permute-start.1
  317.9 11.5 slice.1851
  329.4 11.8 slice.1849
  344.9 11.9 slice.1847
  356.9 11.8 slice.1845
  390.3 9.1 collective-permute-start.14
  426.1 424.3 %while.137 = (s32[]{:T(128)}, bf16[1,2,128,8,128]{4,3,2,1,0:T(8,128)(2,1)}, bf16[1,2,128,8,128]{4,3,2,1,0:T(8,128)(2,1)}, f32[1,4,128,8,2,128]{5,4,3,0,2,1:T(2,1...) while((s32[]{:T(128)}, ...), condition=%wide.region_16.17_spmd.clone.clone, body=%wide.region_0.16_spmd.clone.clone.sunk | while | flops 1327627008 | bytes 139415504 | solution.py:269
  851.7 5.8 scatter-add.44
  859.0 5.6 collective-permute-start.17
  864.6 7.6 collective-permute-done.16
  878.0 8.1 collective-permute-done.18
  893.3 6.1 scatter-add.45
  902.4 8.0 collective-permute-done.19
  912.0 13.4 %collective-permute-start.21 = (bf16[1,64,2048]{1,2,0:T(8,128)(2,1)S(1)}, bf16[1,64,2048]{1,2,0:T(8,128)(2,1)S(1)}, u32[]{:S(2)}, u32[]{:S(2)}) collective-permute-start(bf16[1,64,2048]{1,2,0:T(8,128)(2,1)S(1)} %select_convert_fusion.2), channel_id=1, source_target_pairs={{0,16},{4,20},{8,24},{12,28},{16,0},{20,4},{24,8},{28,12},{32,48},... | collective-permute-start | bytes 786440 | tf_op jit(solution)/shard_map/ppermute | solution.py:18
  928.3 4.6 collective-permute-done.21
  940.1 6.1 scatter-add.46
  949.2 9.5 collective-permute-done.22
  960.3 9.3 collective-permute-start.24
  988.1 8.6 scatter-add.49
  1001.5 5.7 collective-permute-done.25
  1009.6 17.7 %collective-permute-start.27 = (bf16[1,64,2048]{1,2,0:T(8,128)(2,1)}, bf16[1,64,2048]{1,2,0:T(8,128)(2,1)}, u32[]{:S(2)}, u32[]{:S(2)}) collective-permute-start(bf16[1,64,2048]{1,2,0:T(8,128)(2,1)} %select_convert_fusion), channel_id=1, source_target_pairs={{0,4},{4,0},{8,12},{12,8},{16,20},{20,16},{24,28},{28,24},{32,36},... | collective-permute-start | bytes 786440 | tf_op jit(solution)/shard_map/ppermute | solution.py:18
  1042.5 4.5 collective-permute-start.28
  1047.0 4.5 slice.2068
  1059.1 5.8 scatter-add.50
  1071.4 4.2 collective-permute-start.30
  1089.2 5.5 copy.821
  1102.5 129.7 %all-reduce.24.cloned.1.call-done = f32[5,4,8,2,128]{4,3,2,1,0:T(2,128)} async-done(((f32[5,4,8,2,128]{4,3,2,1,0:T(2,128)}), f32[5,4,8,2,128]{4,3,2,1,0:T(2,128)}) %all-reduce.24.cloned.1.call-update) | async-done | bytes 163856 | tf_op jit(solution)/shard_map/psum | solution.py:336
  (1171 shorter events, 635.0 us)
Async XLA Ops:
  7.2 1225.0 %all-reduce.24.cloned.1.call-start = ((), (), s32[]{:S(2)}) async-start(), calls=%async_computation | async-start | bytes 327680 | tf_op jit(solution)/shard_map/psum | solution.py:336
  10.7 45.3 %collective-permute-start = (bf16[1,128,2048]{1,2,0:T(8,128)(2,1)S(1)}, bf16[1,128,2048]{1,2,0:T(8,128)(2,1)S(1)}, u32[]{:S(2)}, u32[]{:S(2)}) collective-permute-start(bf16[1,128,2048]{1,2,0:T(8,128)(2,1)S(1)} %get-tuple-element.1887), channel_id=1, source_target_pairs={{0,4},{4,8},{8,12},{12,16},{16,20},{20,24},{24,28},{28,32},{32,36}... | collective-permute-start | bytes 1572872 | tf_op jit(solution)/shard_map/ppermute | solution.py:14
  35.5 65.5 %copy-start.38 = (bf16[1,128,2048]{1,2,0:T(8,128)(2,1)}, bf16[1,128,2048]{1,2,0:T(8,128)(2,1)S(1)}, u32[]{:S(2)}) copy-start(bf16[1,128,2048]{1,2,0:T(8,128)(2,1)S(1)} %slice.1813) | copy-start | bytes 1572868
  55.9 98.4 %copy-start.86 = (f32[1,1,8,2,128]{4,3,2,1,0:T(2,128)}, f32[1,1,8,2,128]{4,3,2,1,0:T(2,128)S(1)}, u32[]{:S(2)}) copy-start(f32[1,1,8,2,128]{4,3,2,1,0:T(2,128)S(1)} %get-tuple-element.1899) | copy-start | bytes 24580
  56.0 98.4 %copy-start.88 = (f32[1,1,8,2,128]{4,3,2,1,0:T(2,128)}, f32[1,1,8,2,128]{4,3,2,1,0:T(2,128)S(1)}, u32[]{:S(2)}) copy-start(f32[1,1,8,2,128]{4,3,2,1,0:T(2,128)S(1)} %get-tuple-element.1900) | copy-start | bytes 24580
  56.0 98.4 %copy-start.90 = (f32[1,1,8,2,128]{4,3,2,1,0:T(2,128)}, f32[1,1,8,2,128]{4,3,2,1,0:T(2,128)S(1)}, u32[]{:S(2)}) copy-start(f32[1,1,8,2,128]{4,3,2,1,0:T(2,128)S(1)} %get-tuple-element.1901) | copy-start | bytes 24580
  56.0 98.4 %copy-start.92 = (f32[1,1,8,2,128]{4,3,2,1,0:T(2,128)}, f32[1,1,8,2,128]{4,3,2,1,0:T(2,128)S(1)}, u32[]{:S(2)}) copy-start(f32[1,1,8,2,128]{4,3,2,1,0:T(2,128)S(1)} %get-tuple-element.1902) | copy-start | bytes 24580
  56.0 312.6 %copy-start.102 = (f32[1,1,8,2,128]{4,3,2,1,0:T(2,128)}, f32[1,1,8,2,128]{4,3,2,1,0:T(2,128)S(1)}, u32[]{:S(2)}) copy-start(f32[1,1,8,2,128]{4,3,2,1,0:T(2,128)S(1)} %get-tuple-element.1894) | copy-start | bytes 24580
  103.9 24.1 %collective-permute-start.2 = (bf16[1,128,2048]{1,2,0:T(8,128)(2,1)S(1)}, bf16[1,128,2048]{1,2,0:T(8,128)(2,1)}, u32[]{:S(2)}, u32[]{:S(2)}) collective-permute-start(bf16[1,128,2048]{1,2,0:T(8,128)(2,1)S(1)} %fusion.161), channel_id=1, source_target_pairs={{0,4},{4,8},{8,12},{12,16},{16,20},{20,24},{24,28},{28,32},{32,36}... | collective-permute-start | bytes 1572872 | tf_op jit(solution)/shard_map/ppermute | solution.py:14
  158.0 3.0 collective-permute-start.4
  162.9 25.5 %collective-permute-start.5 = (bf16[1,128,2048]{1,2,0:T(8,128)(2,1)S(1)}, bf16[1,128,2048]{1,2,0:T(8,128)(2,1)}, u32[]{:S(2)}, u32[]{:S(2)}) collective-permute-start(bf16[1,128,2048]{1,2,0:T(8,128)(2,1)S(1)} %maximum_select_fusion), channel_id=1, source_target_pairs={{0,8},{4,12},{8,16},{12,20},{16,24},{20,28},{24,32},{28,36},{32,40... | collective-permute-start | bytes 1572872 | tf_op jit(solution)/shard_map/ppermute | solution.py:14
  166.4 48.6 %copy-start.94 = (f32[1,1,8,2,128]{4,3,2,1,0:T(2,128)}, f32[1,1,8,2,128]{4,3,2,1,0:T(2,128)S(1)}, u32[]{:S(2)}) copy-start(f32[1,1,8,2,128]{4,3,2,1,0:T(2,128)S(1)} %get-tuple-element.1904) | copy-start | bytes 24580
  166.4 48.6 %copy-start.96 = (f32[1,1,8,2,128]{4,3,2,1,0:T(2,128)}, f32[1,1,8,2,128]{4,3,2,1,0:T(2,128)S(1)}, u32[]{:S(2)}) copy-start(f32[1,1,8,2,128]{4,3,2,1,0:T(2,128)S(1)} %get-tuple-element.1905) | copy-start | bytes 24580
  166.4 48.5 %copy-start.98 = (f32[1,1,8,2,128]{4,3,2,1,0:T(2,128)}, f32[1,1,8,2,128]{4,3,2,1,0:T(2,128)S(1)}, u32[]{:S(2)}) copy-start(f32[1,1,8,2,128]{4,3,2,1,0:T(2,128)S(1)} %get-tuple-element.1906) | copy-start | bytes 24580
  166.4 121.0 %copy-start.104 = (f32[1,1,8,2,128]{4,3,2,1,0:T(2,128)}, f32[1,1,8,2,128]{4,3,2,1,0:T(2,128)S(1)}, u32[]{:S(2)}) copy-start(f32[1,1,8,2,128]{4,3,2,1,0:T(2,128)S(1)} %get-tuple-element.1908) | copy-start | bytes 24580
  166.4 121.0 %copy-start.106 = (f32[1,1,8,2,128]{4,3,2,1,0:T(2,128)}, f32[1,1,8,2,128]{4,3,2,1,0:T(2,128)S(1)}, u32[]{:S(2)}) copy-start(f32[1,1,8,2,128]{4,3,2,1,0:T(2,128)S(1)} %get-tuple-element.1909) | copy-start | bytes 24580
  166.4 121.0 %copy-start.108 = (f32[1,1,8,2,128]{4,3,2,1,0:T(2,128)}, f32[1,1,8,2,128]{4,3,2,1,0:T(2,128)S(1)}, u32[]{:S(2)}) copy-start(f32[1,1,8,2,128]{4,3,2,1,0:T(2,128)S(1)} %get-tuple-element.1910) | copy-start | bytes 24580
  166.4 121.0 %copy-start.110 = (f32[1,1,8,2,128]{4,3,2,1,0:T(2,128)}, f32[1,1,8,2,128]{4,3,2,1,0:T(2,128)S(1)}, u32[]{:S(2)}) copy-start(f32[1,1,8,2,128]{4,3,2,1,0:T(2,128)S(1)} %get-tuple-element.1911) | copy-start | bytes 24580
  166.4 202.2 %copy-start.112 = (f32[1,1,8,2,128]{4,3,2,1,0:T(2,128)}, f32[1,1,8,2,128]{4,3,2,1,0:T(2,128)S(1)}, u32[]{:S(2)}) copy-start(f32[1,1,8,2,128]{4,3,2,1,0:T(2,128)S(1)} %get-tuple-element.1903) | copy-start | bytes 24580
  218.8 13.0 %collective-permute-start.7 = (bf16[1,64,2048]{1,2,0:T(8,128)(2,1)}, bf16[1,64,2048]{1,2,0:T(8,128)(2,1)S(1)}, u32[]{:S(2)}, u32[]{:S(2)}) collective-permute-start(bf16[1,64,2048]{1,2,0:T(8,128)(2,1)} %fusion.177), channel_id=1, source_target_pairs={{0,8},{4,12},{8,0},{12,4},{16,24},{20,28},{24,16},{28,20},{32,40},... | collective-permute-start | bytes 786440 | tf_op jit(solution)/shard_map/ppermute | solution.py:18
  233.6 27.5 %collective-permute-start.8 = (bf16[1,128,2048]{1,2,0:T(8,128)(2,1)S(1)}, bf16[1,128,2048]{1,2,0:T(8,128)(2,1)}, u32[]{:S(2)}, u32[]{:S(2)}) collective-permute-start(bf16[1,128,2048]{1,2,0:T(8,128)(2,1)S(1)} %maximum_select_fusion.1), channel_id=1, source_target_pairs={{0,16},{4,20},{8,24},{12,28},{16,32},{20,36},{24,40},{28,44},{32,4... | collective-permute-start | bytes 1572872 | tf_op jit(solution)/shard_map/ppermute | solution.py:14
  291.4 13.4 %collective-permute-start.10 = (bf16[1,64,2048]{1,2,0:T(8,128)(2,1)}, bf16[1,64,2048]{1,2,0:T(8,128)(2,1)S(1)}, u32[]{:S(2)}, u32[]{:S(2)}) collective-permute-start(bf16[1,64,2048]{1,2,0:T(8,128)(2,1)} %fusion.185), channel_id=1, source_target_pairs={{0,16},{4,20},{8,24},{12,28},{16,0},{20,4},{24,8},{28,12},{32,48},... | collective-permute-start | bytes 786440 | tf_op jit(solution)/shard_map/ppermute | solution.py:18
  307.4 33.8 %collective-permute-start.11 = (bf16[1,128,2048]{1,2,0:T(8,128)(2,1)}, bf16[1,128,2048]{1,2,0:T(8,128)(2,1)}, u32[]{:S(2)}, u32[]{:S(2)}) collective-permute-start(bf16[1,128,2048]{1,2,0:T(8,128)(2,1)} %maximum_select_fusion.2), channel_id=1, source_target_pairs={{0,32},{4,36},{8,40},{12,44},{16,48},{20,52},{24,56},{28,60},{32,6... | collective-permute-start | bytes 1572872 | tf_op jit(solution)/shard_map/ppermute | solution.py:14
  310.9 78.1 %collective-permute-start.1 = (bf16[1,128,2048]{1,2,0:T(8,128)(2,1)}, bf16[1,128,2048]{1,2,0:T(8,128)(2,1)}, u32[]{:S(2)}, u32[]{:S(2)}) collective-permute-start(bf16[1,128,2048]{1,2,0:T(8,128)(2,1)} %get-tuple-element.1888), channel_id=1, source_target_pairs={{4,0},{8,4},{12,8},{16,12},{20,16},{24,20},{28,24},{32,28},{36,32}... | collective-permute-start | bytes 1572872 | tf_op jit(solution)/shard_map/ppermute | solution.py:14
  315.8 52.8 %copy-start.76 = (f32[1,1,8,2,128]{4,3,2,1,0:T(2,128)}, f32[1,1,8,2,128]{4,3,2,1,0:T(2,128)S(1)}, u32[]{:S(2)}) copy-start(f32[1,1,8,2,128]{4,3,2,1,0:T(2,128)S(1)} %get-tuple-element.1913) | copy-start | bytes 24580
  315.8 74.5 %collective-permute-start.3 = (bf16[1,128,2048]{1,2,0:T(8,128)(2,1)S(1)}, bf16[1,128,2048]{1,2,0:T(8,128)(2,1)}, u32[]{:S(2)}, u32[]{:S(2)}) collective-permute-start(bf16[1,128,2048]{1,2,0:T(8,128)(2,1)S(1)} %fusion.161), channel_id=1, source_target_pairs={{4,0},{8,4},{12,8},{16,12},{20,16},{24,20},{28,24},{32,28},{36,32}... | collective-permute-start | bytes 1572872 | tf_op jit(solution)/shard_map/ppermute | solution.py:14
  372.6 12.1 collective-permute-start.13
  380.5 34.4 %collective-permute-start.6 = (bf16[1,128,2048]{1,2,0:T(8,128)(2,1)S(1)}, bf16[1,128,2048]{1,2,0:T(8,128)(2,1)}, u32[]{:S(2)}, u32[]{:S(2)}) collective-permute-start(bf16[1,128,2048]{1,2,0:T(8,128)(2,1)S(1)} %maximum_select_fusion), channel_id=1, source_target_pairs={{8,0},{12,4},{16,8},{20,12},{24,16},{28,20},{32,24},{36,28},{40,32... | collective-permute-start | bytes 1572872 | tf_op jit(solution)/shard_map/ppermute | solution.py:14
  381.8 33.1 %collective-permute-start.9 = (bf16[1,128,2048]{1,2,0:T(8,128)(2,1)S(1)}, bf16[1,128,2048]{1,2,0:T(8,128)(2,1)}, u32[]{:S(2)}, u32[]{:S(2)}) collective-permute-start(bf16[1,128,2048]{1,2,0:T(8,128)(2,1)S(1)} %maximum_select_fusion.1), channel_id=1, source_target_pairs={{16,0},{20,4},{24,8},{28,12},{32,16},{36,20},{40,24},{44,28},{48,3... | collective-permute-start | bytes 1572872 | tf_op jit(solution)/shard_map/ppermute | solution.py:14
  384.7 30.2 %collective-permute-start.12 = (bf16[1,128,2048]{1,2,0:T(8,128)(2,1)}, bf16[1,128,2048]{1,2,0:T(8,128)(2,1)}, u32[]{:S(2)}, u32[]{:S(2)}) collective-permute-start(bf16[1,128,2048]{1,2,0:T(8,128)(2,1)} %maximum_select_fusion.2), channel_id=1, source_target_pairs={{32,0},{36,4},{40,8},{44,12},{48,16},{52,20},{56,24},{60,28},{64,3... | collective-permute-start | bytes 1572872 | tf_op jit(solution)/shard_map/ppermute | solution.py:14
  389.0 25.9 %collective-permute-start.15 = (bf16[1,128,2048]{1,2,0:T(8,128)(2,1)}, bf16[1,128,2048]{1,2,0:T(8,128)(2,1)}, u32[]{:S(2)}, u32[]{:S(2)}) collective-permute-start(bf16[1,128,2048]{1,2,0:T(8,128)(2,1)} %maximum_select_fusion.3), channel_id=1, source_target_pairs={{64,0},{68,4},{72,8},{76,12},{80,16},{84,20},{88,24},{92,28},{96,3... | collective-permute-start | bytes 1572872 | tf_op jit(solution)/shard_map/ppermute | solution.py:14
  390.3 24.6 %collective-permute-start.14 = (bf16[1,128,2048]{1,2,0:T(8,128)(2,1)}, bf16[1,128,2048]{1,2,0:T(8,128)(2,1)}, u32[]{:S(2)}, u32[]{:S(2)}) collective-permute-start(bf16[1,128,2048]{1,2,0:T(8,128)(2,1)} %maximum_select_fusion.3), channel_id=1, source_target_pairs={{0,64},{4,68},{8,72},{12,76},{16,80},{20,84},{24,88},{28,92},{32,9... | collective-permute-start | bytes 1572872 | tf_op jit(solution)/shard_map/ppermute | solution.py:14
  857.6 14.6 %collective-permute-start.16 = (bf16[1,128,2048]{1,2,0:T(8,128)(2,1)}, bf16[1,128,2048]{1,2,0:T(8,128)(2,1)S(1)}, u32[]{:S(2)}, u32[]{:S(2)}) collective-permute-start(bf16[1,128,2048]{1,2,0:T(8,128)(2,1)} %scatter-add.44), channel_id=1, source_target_pairs={{64,0},{68,4},{72,8},{76,12},{80,16},{84,20},{88,24},{92,28},{96,3... | collective-permute-start | bytes 1572872 | tf_op jit(solution)/shard_map/ppermute | solution.py:14
  859.0 13.9 %collective-permute-start.17 = (bf16[1,128,2048]{1,2,0:T(8,128)(2,1)S(1)}, bf16[1,128,2048]{1,2,0:T(8,128)(2,1)S(1)}, u32[]{:S(2)}, u32[]{:S(2)}) collective-permute-start(bf16[1,128,2048]{1,2,0:T(8,128)(2,1)S(1)} %bitcast.1758), channel_id=1, source_target_pairs={{0,64},{4,68},{8,72},{12,76},{16,80},{20,84},{24,88},{28,92},{32,9... | collective-permute-start | bytes 1572872 | tf_op jit(solution)/shard_map/ppermute | solution.py:14
  873.2 12.9 %collective-permute-start.18 = (bf16[1,64,2048]{1,2,0:T(8,128)(2,1)S(1)}, bf16[1,64,2048]{1,2,0:T(8,128)(2,1)S(1)}, u32[]{:S(2)}, u32[]{:S(2)}) collective-permute-start(bf16[1,64,2048]{1,2,0:T(8,128)(2,1)S(1)} %select_convert_fusion.3), channel_id=1, source_target_pairs={{0,32},{4,36},{8,40},{12,44},{16,48},{20,52},{24,56},{28,60},{32,0... | collective-permute-start | bytes 786440 | tf_op jit(solution)/shard_map/ppermute | solution.py:18
  875.1 27.3 %collective-permute-start.20 = (bf16[1,128,2048]{1,2,0:T(8,128)(2,1)}, bf16[1,128,2048]{1,2,0:T(8,128)(2,1)}, u32[]{:S(2)}, u32[]{:S(2)}) collective-permute-start(bf16[1,128,2048]{1,2,0:T(8,128)(2,1)} %bitcast.41), channel_id=1, source_target_pairs={{0,32},{4,36},{8,40},{12,44},{16,48},{20,52},{24,56},{28,60},{32,6... | collective-permute-start | bytes 1572872 | tf_op jit(solution)/shard_map/ppermute | solution.py:14
  900.2 10.2 collective-permute-start.19
  912.0 20.8 %collective-permute-start.21 = (bf16[1,64,2048]{1,2,0:T(8,128)(2,1)S(1)}, bf16[1,64,2048]{1,2,0:T(8,128)(2,1)S(1)}, u32[]{:S(2)}, u32[]{:S(2)}) collective-permute-start(bf16[1,64,2048]{1,2,0:T(8,128)(2,1)S(1)} %select_convert_fusion.2), channel_id=1, source_target_pairs={{0,16},{4,20},{8,24},{12,28},{16,0},{20,4},{24,8},{28,12},{32,48},... | collective-permute-start | bytes 786440 | tf_op jit(solution)/shard_map/ppermute | solution.py:18
  925.4 23.9 %collective-permute-start.23 = (bf16[1,128,2048]{1,2,0:T(8,128)(2,1)}, bf16[1,128,2048]{1,2,0:T(8,128)(2,1)}, u32[]{:S(2)}, u32[]{:S(2)}) collective-permute-start(bf16[1,128,2048]{1,2,0:T(8,128)(2,1)} %bitcast.46), channel_id=1, source_target_pairs={{0,16},{4,20},{8,24},{12,28},{16,32},{20,36},{24,40},{28,44},{32,4... | collective-permute-start | bytes 1572872 | tf_op jit(solution)/shard_map/ppermute | solution.py:14
  947.0 11.7 collective-permute-start.22
  960.3 15.9 %collective-permute-start.24 = (bf16[1,64,2048]{1,2,0:T(8,128)(2,1)S(1)}, bf16[1,64,2048]{1,2,0:T(8,128)(2,1)S(1)}, u32[]{:S(2)}, u32[]{:S(2)}) collective-permute-start(bf16[1,64,2048]{1,2,0:T(8,128)(2,1)S(1)} %select_convert_fusion.1), channel_id=1, source_target_pairs={{0,8},{4,12},{8,0},{12,4},{16,24},{20,28},{24,16},{28,20},{32,40},... | collective-permute-start | bytes 786440 | tf_op jit(solution)/shard_map/ppermute | solution.py:18
  969.7 31.8 %collective-permute-start.26 = (bf16[1,128,2048]{1,2,0:T(8,128)(2,1)S(1)}, bf16[1,128,2048]{1,2,0:T(8,128)(2,1)}, u32[]{:S(2)}, u32[]{:S(2)}) collective-permute-start(bf16[1,128,2048]{1,2,0:T(8,128)(2,1)S(1)} %bitcast.1723), channel_id=1, source_target_pairs={{0,8},{4,12},{8,16},{12,20},{16,24},{20,28},{24,32},{28,36},{32,40... | collective-permute-start | bytes 1572872 | tf_op jit(solution)/shard_map/ppermute | solution.py:14
  996.8 10.4 collective-permute-start.25
  1009.6 41.9 %collective-permute-start.27 = (bf16[1,64,2048]{1,2,0:T(8,128)(2,1)}, bf16[1,64,2048]{1,2,0:T(8,128)(2,1)}, u32[]{:S(2)}, u32[]{:S(2)}) collective-permute-start(bf16[1,64,2048]{1,2,0:T(8,128)(2,1)} %select_convert_fusion), channel_id=1, source_target_pairs={{0,4},{4,0},{8,12},{12,8},{16,20},{20,16},{24,28},{28,24},{32,36},... | collective-permute-start | bytes 786440 | tf_op jit(solution)/shard_map/ppermute | solution.py:18
  1042.5 37.8 %collective-permute-start.28 = (bf16[1,128,2048]{1,2,0:T(8,128)(2,1)}, bf16[1,128,2048]{1,2,0:T(8,128)(2,1)}, u32[]{:S(2)}, u32[]{:S(2)}) collective-permute-start(bf16[1,128,2048]{1,2,0:T(8,128)(2,1)} %copy.1124), channel_id=1, source_target_pairs={{0,4},{4,8},{8,12},{12,16},{16,20},{20,24},{24,28},{28,32},{32,36}... | collective-permute-start | bytes 1572872 | tf_op jit(solution)/shard_map/ppermute | solution.py:14
  1064.9 15.4 %collective-permute-start.29 = (bf16[1,128,2048]{1,2,0:T(8,128)(2,1)}, bf16[1,128,2048]{1,2,0:T(8,128)(2,1)}, u32[]{:S(2)}, u32[]{:S(2)}) collective-permute-start(bf16[1,128,2048]{1,2,0:T(8,128)(2,1)} %scatter-add.50), channel_id=1, source_target_pairs={{4,0},{8,4},{12,8},{16,12},{20,16},{24,20},{28,24},{32,28},{36,32}... | collective-permute-start | bytes 1572872 | tf_op jit(solution)/shard_map/ppermute | solution.py:14
  1071.4 29.8 %collective-permute-start.30 = (bf16[1,128,2048]{2,1,0:T(8,128)(2,1)}, bf16[1,128,2048]{2,1,0:T(8,128)(2,1)}, u32[]{:S(2)}, u32[]{:S(2)}) collective-permute-start(bf16[1,128,2048]{2,1,0:T(8,128)(2,1)} %copy.823), channel_id=1, source_target_pairs={{0,4},{4,8},{8,12},{12,16},{16,20},{20,24},{24,28},{28,32},{32,36}... | collective-permute-start | bytes 1572872 | tf_op jit(solution)/shard_map/ppermute | solution.py:14
  1097.3 137.7 %collective-permute-start.31 = (bf16[1,128,2048]{2,1,0:T(8,128)(2,1)S(1)}, bf16[1,128,2048]{2,1,0:T(8,128)(2,1)S(1)}, u32[]{:S(2)}, u32[]{:S(2)}) collective-permute-start(bf16[1,128,2048]{2,1,0:T(8,128)(2,1)S(1)} %copy.824), channel_id=1, source_target_pairs={{4,0},{8,4},{12,8},{16,12},{20,16},{24,20},{28,24},{32,28},{36,32}... | collective-permute-start | bytes 1572872 | tf_op jit(solution)/shard_map/ppermute | solution.py:14
  (236 other events, 2402.6 us)
Sparse Core Ops, SparseCore 0:
  1084.6 147.5 all-reduce.23
where the time goes:
time: 1260 us; the launch traced here: 1240 us
  local copies, waits for them, and re-layouts  460 us (37%)
  matrix products  290 us (23%)
  waiting for transfers between devices  207 us (16%)
  other arithmetic  151 us (12%)
  starting transfers between devices  117 us (9%)
  between operations  16 us (1%)
    slice x15, local copies, waits for them, and re-layouts, coarsen(): extended[:, offset:offset + 2 * out_rows:2].astype(jnp.float32)  198 us
    psum x1, waiting for transfers between devices, per_device(): lax.psum(jnp.stack(weight_grads), ('seq', 'dp'))  130 us
    dot_general x52, matrix products, head_group(): jnp.einsum('bnrqhe,bnkhe->bnrhqk', q_view, key_blocks[..., 0, :], preferr...  75.9 us
    ppermute x24, starting transfers between devices, passed_along(): lax.ppermute(value, axis, [(source, source + steps) for source in range(i...  72 us
    slice x5, local copies, waits for them, and re-layouts, coarsen(): summed = weight[0] * extended[:, 0:2 * out_rows:2].astype(jnp.float32)  68.5 us
    dot_general x52, matrix products, head_group(): jnp.einsum('bnrhqk,bnkhe->bnrqhe', p_slice, key_blocks[..., 1, :], prefer...  50.2 us
    dot_general x52, matrix products, head_group(): jnp.einsum('bnrqhe,bnkhe->bnrhqk', do_view, key_blocks[..., 1, :], prefer...  45.6 us
    ppermute x8, waiting for transfers between devices, partner_2(): lax.ppermute(array, axis, [(i, i ^ 1 << distance) for i in range(lax.axis...  45.3 us
  transfers between devices with their start and end apart: 33, of which 13 were waited for; matrix products, arithmetic and copies ran while one was open for 25% of the time, Pallas kernels for 0%

commit v1 on v0

--- a/solution.py
+++ b/solution.py
@@ -333,9 +333,10 @@
     grad_value = (
         grad_pairs[:, :, :, 1, :].reshape(seqs_dev, tok_rows, feat_width).astype(jnp.bfloat16)
     )
-    weight_sum = lax.psum(jnp.stack(weight_grads), ("seq", "dp")).reshape(
-        levels, 4, head_count, 2, head_size
-    )
+    use_core = lambda incoming_x: jnp.sum(
+        jax.lax.all_gather(incoming_x, axis_name=("seq", "dp")), 0
+    )
+    weight_sum = use_core(jnp.stack(weight_grads)).reshape(levels, 4, head_count, 2, head_size)
     grad_conv_key = weight_sum[:, :, :, 0, :].reshape(levels, 4, feat_width)
     grad_conv_value = weight_sum[:, :, :, 1, :].reshape(levels, 4, feat_width)
     return (attended, grad_query, grad_key, grad_value, grad_conv_key, grad_conv_value)

time: 1260 us -> 1220 us (0.968)
  waiting for transfers between devices: 207 us -> 136 us
  matrix products: 290 us -> 314 us
  local copies, waits for them, and re-layouts: 460 us -> 482 us
  other arithmetic: 151 us -> 134 us
    psum x1 -> x0, waiting for transfers between devices: 130 us -> none  [per_device(): lax.psum(jnp.stack(weight_grads), ('seq', 'dp'))]
    all_gather x0 -> x1, waiting for transfers between devices: none -> 52.9 us  [per_device(): jax.lax.all_gather(incoming_x, axis_name=('seq', 'dp'))]
    dot_general x52, matrix products: 45.6 us -> 92.5 us  [head_group(): jnp.einsum('bnrqhe,bnkhe->bnrhqk', do_view, key_blocks[..., 1, :], prefer...]
    dot_general x52, matrix products: 37.6 us -> 11.9 us  [head_group(): jnp.einsum('bnrhqk,bnrqhe->bnkhe', p_slice, do_view, preferred_element_ty...]
    while x360 -> x128, local copies, waits for them, and re-layouts: 14.6 us -> 33.8 us
    dot_general x52, matrix products: 35.7 us -> 22.6 us  [head_group(): jnp.einsum('bnrhqk,bnrqhe->bnkhe', ds_slice, q_view, preferred_element_ty...]
    unnamed x189 -> x195, local copies, waits for them, and re-layouts: 33.6 us -> 37.7 us
  transfers between devices with their start and end apart: 33 -> 33, of which waited for: 13 -> 14; matrix products, arithmetic and copies ran while one was open for 25% -> 25% of each run, Pallas kernels for 0% -> 0%
where the time goes in v1:
time: 1220 us; the launch traced here: 1200 us
  local copies, waits for them, and re-layouts  482 us (40%)
  matrix products  314 us (26%)
  waiting for transfers between devices  136 us (11%)
  other arithmetic  134 us (11%)
  starting transfers between devices  118 us (10%)
  between operations  16 us (1%)
    slice x15, local copies, waits for them, and re-layouts, coarsen(): extended[:, offset:offset + 2 * out_rows:2].astype(jnp.float32)  199 us
    dot_general x52, matrix products, head_group(): jnp.einsum('bnrqhe,bnkhe->bnrhqk', do_view, key_blocks[..., 1, :], prefer...  92.5 us
    dot_general x52, matrix products, head_group(): jnp.einsum('bnrqhe,bnkhe->bnrhqk', q_view, key_blocks[..., 0, :], preferr...  88 us
    ppermute x24, starting transfers between devices, passed_along(): lax.ppermute(value, axis, [(source, source + steps) for source in range(i...  73.4 us
    slice x5, local copies, waits for them, and re-layouts, coarsen(): summed = weight[0] * extended[:, 0:2 * out_rows:2].astype(jnp.float32)  67.6 us
    all_gather x1, waiting for transfers between devices, per_device(): jax.lax.all_gather(incoming_x, axis_name=('seq', 'dp'))  52.9 us
    dot_general x52, matrix products, head_group(): jnp.einsum('bnrhqk,bnkhe->bnrqhe', ds_slice, key_blocks[..., 0, :], prefe...  51.6 us
    dot_general x52, matrix products, head_group(): jnp.einsum('bnrhqk,bnkhe->bnrqhe', p_slice, key_blocks[..., 1, :], prefer...  47.7 us
  transfers between devices with their start and end apart: 33, of which 14 were waited for; matrix products, arithmetic and copies ran while one was open for 25% of the time, Pallas kernels for 0%

profile of v1, /device:TPU:1, one launch (start us, length us, event | category | flops | bytes accessed | tf_op | source)
XLA Modules:
  0.0 1203.0 jit_solution(667915682794034222)
XLA Ops:
  10.7 4.5 collective-permute-start
  15.2 20.2 %slice.1813 = bf16[1,128,2048]{1,2,0:T(8,128)(2,1)S(1)} slice(bf16[1,256,2048]{1,2,0:T(8,128)(2,1)S(1)} %bitcast.1717), slice={[0:1:1], [0:256:2], [0:2048:1]} | slice | bytes 1048576 | tf_op jit(solution)/shard_map/slice | solution.py:25
  35.5 20.2 %slice.1815 = bf16[1,128,2048]{1,2,0:T(8,128)(2,1)S(1)} slice(bf16[1,256,2048]{1,2,0:T(8,128)(2,1)S(1)} %bitcast.1718), slice={[0:1:1], [1:256:2], [0:2048:1]} | slice | bytes 1048576 | tf_op jit(solution)/shard_map/slice | solution.py:25
  58.7 20.9 %slice.1809 = bf16[1,128,2048]{1,2,0:T(8,128)(2,1)S(1)} slice(bf16[1,258,2048]{1,2,0:T(8,128)(2,1)} %pad_maximum_fusion.14), slice={[0:1:1], [0:256:2], [0:2048:1]} | slice | bytes 1048576 | tf_op jit(solution)/shard_map/slice | solution.py:23
  79.6 21.4 %slice.1811 = bf16[1,128,2048]{1,2,0:T(8,128)(2,1)} slice(bf16[1,258,2048]{1,2,0:T(8,128)(2,1)} %pad_maximum_fusion.14), slice={[0:1:1], [1:257:2], [0:2048:1]} | slice | bytes 1048576 | tf_op jit(solution)/shard_map/slice | solution.py:25
  106.1 10.9 slice.1822
  117.0 11.0 slice.1824
  130.9 11.4 slice.1818
  142.4 12.1 %slice.1820 = bf16[1,64,2048]{1,2,0:T(8,128)(2,1)} slice(bf16[1,130,2048]{1,2,0:T(8,128)(2,1)} %pad_maximum_fusion.17), slice={[0:1:1], [1:129:2], [0:2048:1]} | slice | bytes 524288 | tf_op jit(solution)/shard_map/slice | solution.py:25
  166.8 10.9 slice.1831
  177.7 11.0 slice.1833
  191.6 11.8 slice.1827
  203.4 11.9 slice.1829
  219.3 12.9 %collective-permute-done.7 = bf16[1,64,2048]{1,2,0:T(8,128)(2,1)S(1)} collective-permute-done((bf16[1,64,2048]{1,2,0:T(8,128)(2,1)}, bf16[1,64,2048]{1,2,0:T(8,128)(2,1)S(1)}, u32[]{:S(2)}, u32[]{:S(2)}) %collective-permute-start.7) | collective-permute-done | bytes 262176 | tf_op jit(solution)/shard_map/ppermute | solution.py:18
  234.0 4.9 collective-permute-start.8
  238.9 10.9 slice.1840
  249.8 11.3 slice.1842
  263.9 11.8 slice.1836
  275.6 11.9 slice.1838
  292.3 12.7 %collective-permute-done.10 = bf16[1,64,2048]{1,2,0:T(8,128)(2,1)S(1)} collective-permute-done((bf16[1,64,2048]{1,2,0:T(8,128)(2,1)}, bf16[1,64,2048]{1,2,0:T(8,128)(2,1)S(1)}, u32[]{:S(2)}, u32[]{:S(2)}) %collective-permute-start.10) | collective-permute-done | bytes 262176 | tf_op jit(solution)/shard_map/ppermute | solution.py:18
  311.1 4.8 collective-permute-start.1
  318.1 11.4 slice.1849
  329.5 11.9 slice.1851
  345.1 11.8 slice.1845
  356.9 11.9 slice.1847
  392.7 9.9 collective-permute-start.14
  430.6 446.4 %while.137 = (s32[]{:T(128)}, bf16[1,2,128,8,128]{4,3,2,1,0:T(8,128)(2,1)}, bf16[1,2,128,8,128]{4,3,2,1,0:T(8,128)(2,1)}, f32[1,4,128,8,2,128]{5,4,3,0,2,1:T(2,1...) while((s32[]{:T(128)}, ...), condition=%wide.region_16.17_spmd.clone.clone, body=%wide.region_0.16_spmd.clone.clone.sunk | while | flops 1327627008 | bytes 128404528 | solution.py:269
  878.3 5.8 scatter-add.44
  885.6 6.3 collective-permute-start.17
  891.9 7.6 collective-permute-done.16
  904.9 8.2 collective-permute-done.18
  920.3 6.1 scatter-add.45
  929.4 8.0 collective-permute-done.19
  939.0 13.6 %collective-permute-start.21 = (bf16[1,64,2048]{1,2,0:T(8,128)(2,1)S(1)}, bf16[1,64,2048]{1,2,0:T(8,128)(2,1)S(1)}, u32[]{:S(2)}, u32[]{:S(2)}) collective-permute-start(bf16[1,64,2048]{1,2,0:T(8,128)(2,1)S(1)} %select_convert_fusion.2), channel_id=1, source_target_pairs={{0,16},{4,20},{8,24},{12,28},{16,0},{20,4},{24,8},{28,12},{32,48},... | collective-permute-start | bytes 786440 | tf_op jit(solution)/shard_map/ppermute | solution.py:18
  955.6 4.5 collective-permute-done.21
  967.4 6.1 scatter-add.46
  976.5 9.6 collective-permute-done.22
  987.6 9.5 collective-permute-start.24
  1010.9 6.1 scatter-add.49
  1019.2 8.2 collective-permute-done.25
  1029.6 17.7 %collective-permute-start.27 = (bf16[1,64,2048]{1,2,0:T(8,128)(2,1)}, bf16[1,64,2048]{1,2,0:T(8,128)(2,1)}, u32[]{:S(2)}, u32[]{:S(2)}) collective-permute-start(bf16[1,64,2048]{1,2,0:T(8,128)(2,1)} %select_convert_fusion), channel_id=1, source_target_pairs={{0,4},{4,0},{8,12},{12,8},{16,20},{20,16},{24,28},{28,24},{32,36},... | collective-permute-start | bytes 786440 | tf_op jit(solution)/shard_map/ppermute | solution.py:18
  1058.2 4.4 collective-permute-start.28
  1070.1 5.8 scatter-add.50
  1090.7 4.5 slice.2068
  1108.6 5.5 copy.821
  1122.1 5.1 collective-permute-done.31
  1130.2 52.9 %all-gather.3.cloned.1.call-done = f32[640,4,2048]{2,1,0:T(4,128)} async-done(((f32[5,4,2048]{2,1,0:T(4,128)}), f32[640,4,2048]{2,1,0:T(4,128)}) %all-gather.3.cloned.1.call-update) | async-done | bytes 20971536 | tf_op jit(solution)/shard_map/all_gather | solution.py:337
  1183.0 10.9 reduce_sum.231
  (946 shorter events, 661.6 us)
Async XLA Ops:
  7.2 1175.9 %all-gather.3.cloned.1.call-start = ((), (), s32[]{:S(2)}) async-start(), calls=%async_computation | async-start | bytes 21135360 | tf_op jit(solution)/shard_map/all_gather | solution.py:337
  10.7 45.3 %collective-permute-start = (bf16[1,128,2048]{1,2,0:T(8,128)(2,1)S(1)}, bf16[1,128,2048]{1,2,0:T(8,128)(2,1)S(1)}, u32[]{:S(2)}, u32[]{:S(2)}) collective-permute-start(bf16[1,128,2048]{1,2,0:T(8,128)(2,1)S(1)} %get-tuple-element.1887), channel_id=1, source_target_pairs={{0,4},{4,8},{8,12},{12,16},{16,20},{20,24},{24,28},{28,32},{32,36}... | collective-permute-start | bytes 1572872 | tf_op jit(solution)/shard_map/ppermute | solution.py:14
  35.5 65.5 %copy-start.19 = (bf16[1,128,2048]{1,2,0:T(8,128)(2,1)}, bf16[1,128,2048]{1,2,0:T(8,128)(2,1)S(1)}, u32[]{:S(2)}) copy-start(bf16[1,128,2048]{1,2,0:T(8,128)(2,1)S(1)} %slice.1813) | copy-start | bytes 1572868
  55.9 98.5 %copy-start.71 = (f32[1,1,8,2,128]{4,3,2,1,0:T(2,128)}, f32[1,1,8,2,128]{4,3,2,1,0:T(2,128)S(1)}, u32[]{:S(2)}) copy-start(f32[1,1,8,2,128]{4,3,2,1,0:T(2,128)S(1)} %get-tuple-element.1899) | copy-start | bytes 24580
  56.0 98.5 %copy-start.73 = (f32[1,1,8,2,128]{4,3,2,1,0:T(2,128)}, f32[1,1,8,2,128]{4,3,2,1,0:T(2,128)S(1)}, u32[]{:S(2)}) copy-start(f32[1,1,8,2,128]{4,3,2,1,0:T(2,128)S(1)} %get-tuple-element.1900) | copy-start | bytes 24580
  56.0 98.5 %copy-start.75 = (f32[1,1,8,2,128]{4,3,2,1,0:T(2,128)}, f32[1,1,8,2,128]{4,3,2,1,0:T(2,128)S(1)}, u32[]{:S(2)}) copy-start(f32[1,1,8,2,128]{4,3,2,1,0:T(2,128)S(1)} %get-tuple-element.1901) | copy-start | bytes 24580
  56.0 98.5 %copy-start.77 = (f32[1,1,8,2,128]{4,3,2,1,0:T(2,128)}, f32[1,1,8,2,128]{4,3,2,1,0:T(2,128)S(1)}, u32[]{:S(2)}) copy-start(f32[1,1,8,2,128]{4,3,2,1,0:T(2,128)S(1)} %get-tuple-element.1902) | copy-start | bytes 24580
  56.0 312.8 %copy-start.87 = (f32[1,1,8,2,128]{4,3,2,1,0:T(2,128)}, f32[1,1,8,2,128]{4,3,2,1,0:T(2,128)S(1)}, u32[]{:S(2)}) copy-start(f32[1,1,8,2,128]{4,3,2,1,0:T(2,128)S(1)} %get-tuple-element.1894) | copy-start | bytes 24580
  103.9 24.1 %collective-permute-start.2 = (bf16[1,128,2048]{1,2,0:T(8,128)(2,1)S(1)}, bf16[1,128,2048]{1,2,0:T(8,128)(2,1)}, u32[]{:S(2)}, u32[]{:S(2)}) collective-permute-start(bf16[1,128,2048]{1,2,0:T(8,128)(2,1)S(1)} %fusion.161), channel_id=1, source_target_pairs={{0,4},{4,8},{8,12},{12,16},{16,20},{20,24},{24,28},{28,32},{32,36}... | collective-permute-start | bytes 1572872 | tf_op jit(solution)/shard_map/ppermute | solution.py:14
  158.1 3.0 collective-permute-start.4
  163.0 25.7 %collective-permute-start.5 = (bf16[1,128,2048]{1,2,0:T(8,128)(2,1)S(1)}, bf16[1,128,2048]{1,2,0:T(8,128)(2,1)}, u32[]{:S(2)}, u32[]{:S(2)}) collective-permute-start(bf16[1,128,2048]{1,2,0:T(8,128)(2,1)S(1)} %maximum_select_fusion), channel_id=1, source_target_pairs={{0,8},{4,12},{8,16},{12,20},{16,24},{20,28},{24,32},{28,36},{32,40... | collective-permute-start | bytes 1572872 | tf_op jit(solution)/shard_map/ppermute | solution.py:14
  166.7 48.6 %copy-start.79 = (f32[1,1,8,2,128]{4,3,2,1,0:T(2,128)}, f32[1,1,8,2,128]{4,3,2,1,0:T(2,128)S(1)}, u32[]{:S(2)}) copy-start(f32[1,1,8,2,128]{4,3,2,1,0:T(2,128)S(1)} %get-tuple-element.1904) | copy-start | bytes 24580
  166.7 48.6 %copy-start.81 = (f32[1,1,8,2,128]{4,3,2,1,0:T(2,128)}, f32[1,1,8,2,128]{4,3,2,1,0:T(2,128)S(1)}, u32[]{:S(2)}) copy-start(f32[1,1,8,2,128]{4,3,2,1,0:T(2,128)S(1)} %get-tuple-element.1905) | copy-start | bytes 24580
  166.7 48.6 %copy-start.83 = (f32[1,1,8,2,128]{4,3,2,1,0:T(2,128)}, f32[1,1,8,2,128]{4,3,2,1,0:T(2,128)S(1)}, u32[]{:S(2)}) copy-start(f32[1,1,8,2,128]{4,3,2,1,0:T(2,128)S(1)} %get-tuple-element.1906) | copy-start | bytes 24580
  166.8 120.8 %copy-start.89 = (f32[1,1,8,2,128]{4,3,2,1,0:T(2,128)}, f32[1,1,8,2,128]{4,3,2,1,0:T(2,128)S(1)}, u32[]{:S(2)}) copy-start(f32[1,1,8,2,128]{4,3,2,1,0:T(2,128)S(1)} %get-tuple-element.1908) | copy-start | bytes 24580
  166.8 120.8 %copy-start.91 = (f32[1,1,8,2,128]{4,3,2,1,0:T(2,128)}, f32[1,1,8,2,128]{4,3,2,1,0:T(2,128)S(1)}, u32[]{:S(2)}) copy-start(f32[1,1,8,2,128]{4,3,2,1,0:T(2,128)S(1)} %get-tuple-element.1909) | copy-start | bytes 24580
  166.8 120.8 %copy-start.93 = (f32[1,1,8,2,128]{4,3,2,1,0:T(2,128)}, f32[1,1,8,2,128]{4,3,2,1,0:T(2,128)S(1)}, u32[]{:S(2)}) copy-start(f32[1,1,8,2,128]{4,3,2,1,0:T(2,128)S(1)} %get-tuple-element.1910) | copy-start | bytes 24580
  166.8 120.8 %copy-start.95 = (f32[1,1,8,2,128]{4,3,2,1,0:T(2,128)}, f32[1,1,8,2,128]{4,3,2,1,0:T(2,128)S(1)}, u32[]{:S(2)}) copy-start(f32[1,1,8,2,128]{4,3,2,1,0:T(2,128)S(1)} %get-tuple-element.1911) | copy-start | bytes 24580
  166.8 202.0 %copy-start.97 = (f32[1,1,8,2,128]{4,3,2,1,0:T(2,128)}, f32[1,1,8,2,128]{4,3,2,1,0:T(2,128)S(1)}, u32[]{:S(2)}) copy-start(f32[1,1,8,2,128]{4,3,2,1,0:T(2,128)S(1)} %get-tuple-element.1903) | copy-start | bytes 24580
  219.1 13.0 %collective-permute-start.7 = (bf16[1,64,2048]{1,2,0:T(8,128)(2,1)}, bf16[1,64,2048]{1,2,0:T(8,128)(2,1)S(1)}, u32[]{:S(2)}, u32[]{:S(2)}) collective-permute-start(bf16[1,64,2048]{1,2,0:T(8,128)(2,1)} %fusion.177), channel_id=1, source_target_pairs={{0,8},{4,12},{8,0},{12,4},{16,24},{20,28},{24,16},{28,20},{32,40},... | collective-permute-start | bytes 786440 | tf_op jit(solution)/shard_map/ppermute | solution.py:18
  234.0 27.2 %collective-permute-start.8 = (bf16[1,128,2048]{1,2,0:T(8,128)(2,1)S(1)}, bf16[1,128,2048]{1,2,0:T(8,128)(2,1)}, u32[]{:S(2)}, u32[]{:S(2)}) collective-permute-start(bf16[1,128,2048]{1,2,0:T(8,128)(2,1)S(1)} %maximum_select_fusion.1), channel_id=1, source_target_pairs={{0,16},{4,20},{8,24},{12,28},{16,32},{20,36},{24,40},{28,44},{32,4... | collective-permute-start | bytes 1572872 | tf_op jit(solution)/shard_map/ppermute | solution.py:14
  291.6 13.4 %collective-permute-start.10 = (bf16[1,64,2048]{1,2,0:T(8,128)(2,1)}, bf16[1,64,2048]{1,2,0:T(8,128)(2,1)S(1)}, u32[]{:S(2)}, u32[]{:S(2)}) collective-permute-start(bf16[1,64,2048]{1,2,0:T(8,128)(2,1)} %fusion.185), channel_id=1, source_target_pairs={{0,16},{4,20},{8,24},{12,28},{16,0},{20,4},{24,8},{28,12},{32,48},... | collective-permute-start | bytes 786440 | tf_op jit(solution)/shard_map/ppermute | solution.py:18
  307.6 33.8 %collective-permute-start.11 = (bf16[1,128,2048]{1,2,0:T(8,128)(2,1)}, bf16[1,128,2048]{1,2,0:T(8,128)(2,1)}, u32[]{:S(2)}, u32[]{:S(2)}) collective-permute-start(bf16[1,128,2048]{1,2,0:T(8,128)(2,1)} %maximum_select_fusion.2), channel_id=1, source_target_pairs={{0,32},{4,36},{8,40},{12,44},{16,48},{20,52},{24,56},{28,60},{32,6... | collective-permute-start | bytes 1572872 | tf_op jit(solution)/shard_map/ppermute | solution.py:14
  311.1 81.6 %collective-permute-start.1 = (bf16[1,128,2048]{1,2,0:T(8,128)(2,1)}, bf16[1,128,2048]{1,2,0:T(8,128)(2,1)}, u32[]{:S(2)}, u32[]{:S(2)}) collective-permute-start(bf16[1,128,2048]{1,2,0:T(8,128)(2,1)} %get-tuple-element.1888), channel_id=1, source_target_pairs={{4,0},{8,4},{12,8},{16,12},{20,16},{24,20},{28,24},{32,28},{36,32}... | collective-permute-start | bytes 1572872 | tf_op jit(solution)/shard_map/ppermute | solution.py:14
  315.9 52.9 %copy-start.61 = (f32[1,1,8,2,128]{4,3,2,1,0:T(2,128)}, f32[1,1,8,2,128]{4,3,2,1,0:T(2,128)S(1)}, u32[]{:S(2)}) copy-start(f32[1,1,8,2,128]{4,3,2,1,0:T(2,128)S(1)} %get-tuple-element.1913) | copy-start | bytes 24580
  316.0 86.7 %collective-permute-start.3 = (bf16[1,128,2048]{1,2,0:T(8,128)(2,1)S(1)}, bf16[1,128,2048]{1,2,0:T(8,128)(2,1)}, u32[]{:S(2)}, u32[]{:S(2)}) collective-permute-start(bf16[1,128,2048]{1,2,0:T(8,128)(2,1)S(1)} %fusion.161), channel_id=1, source_target_pairs={{4,0},{8,4},{12,8},{16,12},{20,16},{24,20},{28,24},{32,28},{36,32}... | collective-permute-start | bytes 1572872 | tf_op jit(solution)/shard_map/ppermute | solution.py:14
  372.8 15.6 %collective-permute-start.13 = (bf16[1,64,2048]{1,2,0:T(8,128)(2,1)}, bf16[1,64,2048]{1,2,0:T(8,128)(2,1)}, u32[]{:S(2)}, u32[]{:S(2)}) collective-permute-start(bf16[1,64,2048]{1,2,0:T(8,128)(2,1)} %fusion.193), channel_id=1, source_target_pairs={{0,32},{4,36},{8,40},{12,44},{16,48},{20,52},{24,56},{28,60},{32,0... | collective-permute-start | bytes 786440 | tf_op jit(solution)/shard_map/ppermute | solution.py:18
  385.8 33.6 %collective-permute-start.6 = (bf16[1,128,2048]{1,2,0:T(8,128)(2,1)S(1)}, bf16[1,128,2048]{1,2,0:T(8,128)(2,1)}, u32[]{:S(2)}, u32[]{:S(2)}) collective-permute-start(bf16[1,128,2048]{1,2,0:T(8,128)(2,1)S(1)} %maximum_select_fusion), channel_id=1, source_target_pairs={{8,0},{12,4},{16,8},{20,12},{24,16},{28,20},{32,24},{36,28},{40,32... | collective-permute-start | bytes 1572872 | tf_op jit(solution)/shard_map/ppermute | solution.py:14
  387.1 32.4 %collective-permute-start.9 = (bf16[1,128,2048]{1,2,0:T(8,128)(2,1)S(1)}, bf16[1,128,2048]{1,2,0:T(8,128)(2,1)}, u32[]{:S(2)}, u32[]{:S(2)}) collective-permute-start(bf16[1,128,2048]{1,2,0:T(8,128)(2,1)S(1)} %maximum_select_fusion.1), channel_id=1, source_target_pairs={{16,0},{20,4},{24,8},{28,12},{32,16},{36,20},{40,24},{44,28},{48,3... | collective-permute-start | bytes 1572872 | tf_op jit(solution)/shard_map/ppermute | solution.py:14
  388.4 31.1 %collective-permute-start.12 = (bf16[1,128,2048]{1,2,0:T(8,128)(2,1)}, bf16[1,128,2048]{1,2,0:T(8,128)(2,1)}, u32[]{:S(2)}, u32[]{:S(2)}) collective-permute-start(bf16[1,128,2048]{1,2,0:T(8,128)(2,1)} %maximum_select_fusion.2), channel_id=1, source_target_pairs={{32,0},{36,4},{40,8},{44,12},{48,16},{52,20},{56,24},{60,28},{64,3... | collective-permute-start | bytes 1572872 | tf_op jit(solution)/shard_map/ppermute | solution.py:14
  392.7 26.8 %collective-permute-start.14 = (bf16[1,128,2048]{1,2,0:T(8,128)(2,1)}, bf16[1,128,2048]{1,2,0:T(8,128)(2,1)}, u32[]{:S(2)}, u32[]{:S(2)}) collective-permute-start(bf16[1,128,2048]{1,2,0:T(8,128)(2,1)} %maximum_select_fusion.3), channel_id=1, source_target_pairs={{0,64},{4,68},{8,72},{12,76},{16,80},{20,84},{24,88},{28,92},{32,9... | collective-permute-start | bytes 1572872 | tf_op jit(solution)/shard_map/ppermute | solution.py:14
  402.6 16.9 %collective-permute-start.15 = (bf16[1,128,2048]{1,2,0:T(8,128)(2,1)}, bf16[1,128,2048]{1,2,0:T(8,128)(2,1)}, u32[]{:S(2)}, u32[]{:S(2)}) collective-permute-start(bf16[1,128,2048]{1,2,0:T(8,128)(2,1)} %maximum_select_fusion.3), channel_id=1, source_target_pairs={{64,0},{68,4},{72,8},{76,12},{80,16},{84,20},{88,24},{92,28},{96,3... | collective-permute-start | bytes 1572872 | tf_op jit(solution)/shard_map/ppermute | solution.py:14
  884.2 15.4 %collective-permute-start.16 = (bf16[1,128,2048]{1,2,0:T(8,128)(2,1)}, bf16[1,128,2048]{1,2,0:T(8,128)(2,1)S(1)}, u32[]{:S(2)}, u32[]{:S(2)}) collective-permute-start(bf16[1,128,2048]{1,2,0:T(8,128)(2,1)} %scatter-add.44), channel_id=1, source_target_pairs={{64,0},{68,4},{72,8},{76,12},{80,16},{84,20},{88,24},{92,28},{96,3... | collective-permute-start | bytes 1572872 | tf_op jit(solution)/shard_map/ppermute | solution.py:14
  885.6 14.6 %collective-permute-start.17 = (bf16[1,128,2048]{1,2,0:T(8,128)(2,1)S(1)}, bf16[1,128,2048]{1,2,0:T(8,128)(2,1)S(1)}, u32[]{:S(2)}, u32[]{:S(2)}) collective-permute-start(bf16[1,128,2048]{1,2,0:T(8,128)(2,1)S(1)} %bitcast.1760), channel_id=1, source_target_pairs={{0,64},{4,68},{8,72},{12,76},{16,80},{20,84},{24,88},{28,92},{32,9... | collective-permute-start | bytes 1572872 | tf_op jit(solution)/shard_map/ppermute | solution.py:14
  900.6 12.5 %collective-permute-start.18 = (bf16[1,64,2048]{1,2,0:T(8,128)(2,1)S(1)}, bf16[1,64,2048]{1,2,0:T(8,128)(2,1)S(1)}, u32[]{:S(2)}, u32[]{:S(2)}) collective-permute-start(bf16[1,64,2048]{1,2,0:T(8,128)(2,1)S(1)} %select_convert_fusion.3), channel_id=1, source_target_pairs={{0,32},{4,36},{8,40},{12,44},{16,48},{20,52},{24,56},{28,60},{32,0... | collective-permute-start | bytes 786440 | tf_op jit(solution)/shard_map/ppermute | solution.py:18
  901.7 27.7 %collective-permute-start.20 = (bf16[1,128,2048]{1,2,0:T(8,128)(2,1)}, bf16[1,128,2048]{1,2,0:T(8,128)(2,1)}, u32[]{:S(2)}, u32[]{:S(2)}) collective-permute-start(bf16[1,128,2048]{1,2,0:T(8,128)(2,1)} %bitcast.41), channel_id=1, source_target_pairs={{0,32},{4,36},{8,40},{12,44},{16,48},{20,52},{24,56},{28,60},{32,6... | collective-permute-start | bytes 1572872 | tf_op jit(solution)/shard_map/ppermute | solution.py:14
  927.3 10.2 collective-permute-start.19
  939.0 21.0 %collective-permute-start.21 = (bf16[1,64,2048]{1,2,0:T(8,128)(2,1)S(1)}, bf16[1,64,2048]{1,2,0:T(8,128)(2,1)S(1)}, u32[]{:S(2)}, u32[]{:S(2)}) collective-permute-start(bf16[1,64,2048]{1,2,0:T(8,128)(2,1)S(1)} %select_convert_fusion.2), channel_id=1, source_target_pairs={{0,16},{4,20},{8,24},{12,28},{16,0},{20,4},{24,8},{28,12},{32,48},... | collective-permute-start | bytes 786440 | tf_op jit(solution)/shard_map/ppermute | solution.py:18
  952.7 23.8 %collective-permute-start.23 = (bf16[1,128,2048]{1,2,0:T(8,128)(2,1)}, bf16[1,128,2048]{1,2,0:T(8,128)(2,1)}, u32[]{:S(2)}, u32[]{:S(2)}) collective-permute-start(bf16[1,128,2048]{1,2,0:T(8,128)(2,1)} %bitcast.46), channel_id=1, source_target_pairs={{0,16},{4,20},{8,24},{12,28},{16,32},{20,36},{24,40},{28,44},{32,4... | collective-permute-start | bytes 1572872 | tf_op jit(solution)/shard_map/ppermute | solution.py:14
  974.3 11.7 collective-permute-start.22
  987.6 16.0 %collective-permute-start.24 = (bf16[1,64,2048]{1,2,0:T(8,128)(2,1)S(1)}, bf16[1,64,2048]{1,2,0:T(8,128)(2,1)S(1)}, u32[]{:S(2)}, u32[]{:S(2)}) collective-permute-start(bf16[1,64,2048]{1,2,0:T(8,128)(2,1)S(1)} %select_convert_fusion.1), channel_id=1, source_target_pairs={{0,8},{4,12},{8,0},{12,4},{16,24},{20,28},{24,16},{28,20},{32,40},... | collective-permute-start | bytes 786440 | tf_op jit(solution)/shard_map/ppermute | solution.py:18
  997.1 22.2 %collective-permute-start.26 = (bf16[1,128,2048]{1,2,0:T(8,128)(2,1)}, bf16[1,128,2048]{1,2,0:T(8,128)(2,1)}, u32[]{:S(2)}, u32[]{:S(2)}) collective-permute-start(bf16[1,128,2048]{1,2,0:T(8,128)(2,1)} %bitcast.51), channel_id=1, source_target_pairs={{0,8},{4,12},{8,16},{12,20},{16,24},{20,28},{24,32},{28,36},{32,40... | collective-permute-start | bytes 1572872 | tf_op jit(solution)/shard_map/ppermute | solution.py:14
  1017.1 10.3 collective-permute-start.25
  1029.6 33.0 %collective-permute-start.27 = (bf16[1,64,2048]{1,2,0:T(8,128)(2,1)}, bf16[1,64,2048]{1,2,0:T(8,128)(2,1)}, u32[]{:S(2)}, u32[]{:S(2)}) collective-permute-start(bf16[1,64,2048]{1,2,0:T(8,128)(2,1)} %select_convert_fusion), channel_id=1, source_target_pairs={{0,4},{4,0},{8,12},{12,8},{16,20},{20,16},{24,28},{28,24},{32,36},... | collective-permute-start | bytes 786440 | tf_op jit(solution)/shard_map/ppermute | solution.py:18
  1058.2 28.0 %collective-permute-start.28 = (bf16[1,128,2048]{1,2,0:T(8,128)(2,1)}, bf16[1,128,2048]{1,2,0:T(8,128)(2,1)}, u32[]{:S(2)}, u32[]{:S(2)}) collective-permute-start(bf16[1,128,2048]{1,2,0:T(8,128)(2,1)} %copy.1125), channel_id=1, source_target_pairs={{0,4},{4,8},{8,12},{12,16},{16,20},{20,24},{24,28},{28,32},{32,36}... | collective-permute-start | bytes 1572872 | tf_op jit(solution)/shard_map/ppermute | solution.py:14
  1075.9 10.8 collective-permute-start.29
  1098.6 22.2 %collective-permute-start.30 = (bf16[1,128,2048]{2,1,0:T(8,128)(2,1)}, bf16[1,128,2048]{2,1,0:T(8,128)(2,1)}, u32[]{:S(2)}, u32[]{:S(2)}) collective-permute-start(bf16[1,128,2048]{2,1,0:T(8,128)(2,1)} %copy.823), channel_id=1, source_target_pairs={{0,4},{4,8},{8,12},{12,16},{16,20},{20,24},{24,28},{28,32},{32,36}... | collective-permute-start | bytes 1572872 | tf_op jit(solution)/shard_map/ppermute | solution.py:14
  1116.7 10.5 collective-permute-start.31
  (123 other events, 1617.3 us)
Sparse Core Ops, SparseCore 0:
  1090.8 92.1 all-gather.2
